TPU v7x, 256 devices: a whole 4x4x8 slice. The times are simulated.
256 devices in a mesh: param: 16 (over x, y), space: 2 (over core), term: 8 (over z).
Axes of the slice: x: 4, y: 4, z: 8, core: 2. Of those that a mesh axis runs over, the one named last changes fastest.
Arguments:
- fields: float32 [128, 2, 8, 128, 128], P('param', None, None, 'space'), may hold values from -4 to 4
- library: int32 [168, 4], P('term'), may hold values from 0 to 6, as said below
- centers_x: int32 [16], replicated, may hold values from 0 to 127
- centers_y: int32 [16], replicated, may hold values from 0 to 127
- centers_t: int32 [4], replicated, may hold values from 0 to 7
- groups: int32 [168], replicated, may hold values from 0 to 23
Outputs:
- coefficients: float32 [128, 2, 168], P(('param', 'term'))
- misfit: float32 [128, 2, 168], P(('param', 'term'))
Inputs may be any that keep to these rules, and one draw needn't show every extreme that they name: `library`: each row (a, b, dx, dy) gives powers a and b of 0 to 6 and derivative orders dx and dy of 0 to 2; rows are distinct, and a = b = 0 only with dx = dy = 0.
All inputs are finite; a program needn't handle non-finite values.
Results may differ from a plain program's by a relative error of at most 0.00011.
Values sent between devices are 32-bit elements; how exact they have to be, the bound alone decides.
A program may use at most 64 MiB of HBM per device.

v0:
```python
import jax
import jax.numpy as jnp
from jax import lax
from jax.sharding import PartitionSpec as P

NX = 128
NY = 128
NT = 8
POWERS = 7
TERMS = 168
TESTS = 1024
RX = 16
RT = 4
GROUPS = 24
highest = lax.Precision.HIGHEST


def space_table(centers, first_row, row_count, extent):
    cell_index = first_row + jnp.arange(row_count, dtype=jnp.int32)
    offset = (cell_index[None, :] - centers[:, None] + extent // 2) % extent - extent // 2
    scaled = offset.astype(jnp.float32) / RX
    bump_base = 1.0 - scaled * scaled
    inside = jnp.abs(scaled) < 1.0
    cube = bump_base * bump_base * bump_base
    bump_value = jnp.where(inside, cube * bump_base, 0.0)
    bump_first = jnp.where(inside, 8.0 * scaled * cube / RX, 0.0)
    bump_second = jnp.where(
        inside, -8.0 * (cube - 6.0 * scaled * scaled * bump_base * bump_base) / (RX * RX), 0.0
    )
    return jnp.stack([bump_value, bump_first, bump_second])


def time_table(centers):
    step_index = jnp.arange(NT, dtype=jnp.int32)
    scaled = (step_index[None, :] - centers[:, None]).astype(jnp.float32) / RT
    bump_base = 1.0 - scaled * scaled
    inside = jnp.abs(scaled) < 1.0
    time_bump = jnp.where(inside, bump_base * bump_base, 0.0)
    time_slope = jnp.where(inside, 4.0 * scaled * bump_base / RT, 0.0)
    return (time_bump, time_slope)


def normalize(gram_matrix):
    diagonal = jnp.diagonal(gram_matrix, axis1=1, axis2=2)
    row_scale = jnp.sqrt(diagonal / TESTS + 1e-06)
    term_scale = row_scale[:, :TERMS]
    correlation = gram_matrix[:, :TERMS, :TERMS] / (
        TESTS * term_scale[:, :, None] * term_scale[:, None, :]
    )
    right_side = gram_matrix[:, TERMS:, :TERMS] / (
        TESTS * term_scale[:, None, :] * row_scale[:, TERMS:, None]
    )
    frobenius = jnp.sqrt(jnp.sum(correlation * correlation, axis=(1, 2)))
    return (correlation, right_side, frobenius)


def group_squares(values, onehot):
    return jnp.dot(jnp.sum(values * values, axis=(0, 1)), onehot, precision=highest)


def shrink(values, totals, onehot):
    threshold = 0.7 * jnp.sqrt(jnp.mean(totals))
    per_term = jnp.dot(onehot, totals, precision=highest)
    factor = jnp.maximum(0.0, 1.0 - threshold / jnp.sqrt(per_term + 1e-12))
    return values * factor


def correlate(correlation, values):
    return jnp.einsum("pij,psj->psi", correlation, values, precision=highest)


def body(fields, library, centers_x, centers_y, centers_t, groups):
    pgroup = fields.shape[0]
    tile_rows = fields.shape[3]
    space_count = lax.axis_size("space")
    term_count = lax.axis_size("term")
    local_terms = library.shape[0]
    row_count = local_terms + 2
    half_tests = TESTS // space_count
    y_table = space_table(centers_y, 0, NY, NY)
    time_bump, time_slope = time_table(centers_t)
    x_table = space_table(centers_x, lax.axis_index("space") * tile_rows, tile_rows, NX)
    share_rows = tile_rows // term_count
    share_start = lax.axis_index("term") * share_rows
    x_share = lax.dynamic_slice_in_dim(x_table[0], share_start, share_rows, 1)
    power_a = library[:, 0]
    power_b = library[:, 1]
    orders = jnp.arange(3, dtype=jnp.int32)
    pick_x = (library[:, 2][:, None] == orders[None, :]).astype(jnp.float32)
    pick_y = (library[:, 3][:, None] == orders[None, :]).astype(jnp.float32)
    x_pick = jnp.einsum("jd,dlx->jlx", pick_x, x_table, precision=highest)
    y_pick = jnp.einsum("jd,dky->jky", pick_y, y_table, precision=highest)

    def tile_integrals(field_pair):
        species_u = field_pair[0]
        species_v = field_pair[1]
        power_u = jnp.ones((local_terms,) + species_u.shape, jnp.float32)
        power_v = jnp.ones((local_terms,) + species_v.shape, jnp.float32)
        for degree in range(1, POWERS):
            power_u = power_u * jnp.where(
                power_a[:, None, None, None] >= degree, species_u[None], 1.0
            )
            power_v = power_v * jnp.where(
                power_b[:, None, None, None] >= degree, species_v[None], 1.0
            )
        monomial = power_u * power_v
        across_y = jnp.einsum("jtxy,jky->jtxk", monomial, y_pick, precision=highest)
        across_t = jnp.einsum("jtxk,rt->jrxk", across_y, time_bump, precision=highest)
        features = jnp.einsum("jrxk,jlx->jrkl", across_t, x_pick, precision=highest).reshape(
            local_terms, TESTS
        )
        share = lax.dynamic_slice_in_dim(field_pair, share_start, share_rows, 2)
        target_y = jnp.einsum("stxy,ky->stxk", share, y_table[0], precision=highest)
        targets = jnp.einsum(
            "stxk,rt,lx->srkl", target_y, time_slope, x_share, precision=highest
        ).reshape(2, TESTS)
        joined = jnp.concatenate([features, targets], axis=0).reshape(
            row_count, space_count, half_tests
        )
        return jnp.swapaxes(joined, 0, 1)

    def fill_param(index, buffer):
        field_pair = lax.dynamic_index_in_dim(fields, index, 0, keepdims=False)
        return lax.dynamic_update_slice_in_dim(
            buffer, tile_integrals(field_pair)[:, None], index, 1
        )

    buffer = jnp.zeros((space_count, pgroup, row_count, half_tests), jnp.float32)
    buffer = lax.fori_loop(0, pgroup, fill_param, buffer)
    received = lax.all_to_all(
        buffer.reshape(space_count * pgroup, row_count, half_tests),
        ("space", "term"),
        split_axis=0,
        concat_axis=1,
        tiled=True,
    )
    blocks = jnp.sum(received.reshape(space_count, term_count, row_count, half_tests), axis=0)
    features_half = blocks[:, :local_terms].reshape(term_count * local_terms, half_tests)
    targets_half = jnp.sum(blocks[:, local_terms:], axis=0)
    half_rows = jnp.concatenate([features_half, targets_half], axis=0)
    whole_rows = lax.all_gather(half_rows, "space", axis=1, tiled=True)
    gram_matrix = jnp.dot(whole_rows, whole_rows.T, precision=highest)[None]
    correlation, right_side, frobenius = normalize(gram_matrix)
    onehot = (groups[:, None] == jnp.arange(GROUPS, dtype=jnp.int32)[None, :]).astype(jnp.float32)
    largest = lax.pmax(jnp.max(frobenius), ("param", "term"))
    step_size = 1.0 / largest
    first_guess = step_size * right_side
    first_sq = lax.psum(group_squares(first_guess, onehot), ("param", "term"))
    first = shrink(first_guess, first_sq, onehot)
    second_guess = first - step_size * (correlate(correlation, first) - right_side)
    second_sq = lax.psum(group_squares(second_guess, onehot), ("param", "term"))
    second = shrink(second_guess, second_sq, onehot)
    coefficients = second / step_size
    misfit = right_side - correlate(correlation, second)
    return (coefficients, misfit)


def solution(mesh):
    return jax.shard_map(
        body,
        mesh=mesh,
        in_specs=(P("param", None, None, "space", None), P("term", None), P(), P(), P(), P()),
        out_specs=(P(("param", "term"), None, None), P(("param", "term"), None, None)),
        check_vma=False,
    )
```

profile of v0, /device:TPU:0, one launch (start us, length us, event | category | flops | bytes accessed | tf_op | source)
XLA Modules:
  0.0 1257.9 jit_solution(2309411352389409611)
XLA Ops:
  4.6 175.0 %while.18 = (s32[]{:T(128)}, f32[2,8,23,512]{3,0,2,1:T(2,128)S(1)}, s32[21,1]{0,1:T(1,128)S(1)}, f32[8,2,8,64,128]{4,3,2,1,0:T(8,128)}, s32[21,1]{0,1:T(1,128)S(...) while((s32[]{:T(128)}, f32[2,8,23,512]{3,0,2,1:T(2,128)S(1)}, ...), condition=%wide.region_1.2_spmd.clone.clone, body=%wide.region_0.1_spmd.clone.clone.sunk | while | flops 324181856 | bytes 4605749 | solution.py:129
  4.6 1.1 dynamic-slice_bitcast_fusion.6
  5.7 16.0 %fusion.203 = f32[21,8,64,16]{2,3,1,0:T(8,128)S(1)} fusion(f32[8,64,128]{2,1,0:T(8,128)S(1)} %get-tuple-element.566, f32[8,64,128]{2,1,0:T(8,128)S(1)} %get-tuple-element.567, pred[21]{0:T(512)(128)(4,1)S(1)} %get-tuple-element.568, pred[21]{0:T(512)(128)(4,1)S(1)} %get-tuple-element.569, pred[21]{0:T(512)(128)(4,1)S(1)} %get-tuple-element.570, ...), kind=kOutput, calls=%fused_computation.4.clone.1 | convolution fusion | flops 295895040 | bytes 1384700 | tf_op jit(solution)/shard_map/while/body/eval_jaxpr/jtxy,jky->jtxk/dot_general | solution.py:107
  21.7 1.6 fusion.204
  26.5 1.1 dynamic-slice_bitcast_fusion.6
  27.6 16.0 %fusion.203 = f32[21,8,64,16]{2,3,1,0:T(8,128)S(1)} fusion(f32[8,64,128]{2,1,0:T(8,128)S(1)} %get-tuple-element.566, f32[8,64,128]{2,1,0:T(8,128)S(1)} %get-tuple-element.567, pred[21]{0:T(512)(128)(4,1)S(1)} %get-tuple-element.568, pred[21]{0:T(512)(128)(4,1)S(1)} %get-tuple-element.569, pred[21]{0:T(512)(128)(4,1)S(1)} %get-tuple-element.570, ...), kind=kOutput, calls=%fused_computation.4.clone.1 | convolution fusion | flops 295895040 | bytes 1384700 | tf_op jit(solution)/shard_map/while/body/eval_jaxpr/jtxy,jky->jtxk/dot_general | solution.py:107
  43.6 1.6 fusion.204
  48.3 1.1 dynamic-slice_bitcast_fusion.6
  49.4 16.0 %fusion.203 = f32[21,8,64,16]{2,3,1,0:T(8,128)S(1)} fusion(f32[8,64,128]{2,1,0:T(8,128)S(1)} %get-tuple-element.566, f32[8,64,128]{2,1,0:T(8,128)S(1)} %get-tuple-element.567, pred[21]{0:T(512)(128)(4,1)S(1)} %get-tuple-element.568, pred[21]{0:T(512)(128)(4,1)S(1)} %get-tuple-element.569, pred[21]{0:T(512)(128)(4,1)S(1)} %get-tuple-element.570, ...), kind=kOutput, calls=%fused_computation.4.clone.1 | convolution fusion | flops 295895040 | bytes 1384700 | tf_op jit(solution)/shard_map/while/body/eval_jaxpr/jtxy,jky->jtxk/dot_general | solution.py:107
  65.4 1.6 fusion.204
  70.2 1.1 dynamic-slice_bitcast_fusion.6
  71.3 16.0 %fusion.203 = f32[21,8,64,16]{2,3,1,0:T(8,128)S(1)} fusion(f32[8,64,128]{2,1,0:T(8,128)S(1)} %get-tuple-element.566, f32[8,64,128]{2,1,0:T(8,128)S(1)} %get-tuple-element.567, pred[21]{0:T(512)(128)(4,1)S(1)} %get-tuple-element.568, pred[21]{0:T(512)(128)(4,1)S(1)} %get-tuple-element.569, pred[21]{0:T(512)(128)(4,1)S(1)} %get-tuple-element.570, ...), kind=kOutput, calls=%fused_computation.4.clone.1 | convolution fusion | flops 295895040 | bytes 1384700 | tf_op jit(solution)/shard_map/while/body/eval_jaxpr/jtxy,jky->jtxk/dot_general | solution.py:107
  87.3 1.6 fusion.204
  92.1 1.1 dynamic-slice_bitcast_fusion.6
  93.1 16.0 %fusion.203 = f32[21,8,64,16]{2,3,1,0:T(8,128)S(1)} fusion(f32[8,64,128]{2,1,0:T(8,128)S(1)} %get-tuple-element.566, f32[8,64,128]{2,1,0:T(8,128)S(1)} %get-tuple-element.567, pred[21]{0:T(512)(128)(4,1)S(1)} %get-tuple-element.568, pred[21]{0:T(512)(128)(4,1)S(1)} %get-tuple-element.569, pred[21]{0:T(512)(128)(4,1)S(1)} %get-tuple-element.570, ...), kind=kOutput, calls=%fused_computation.4.clone.1 | convolution fusion | flops 295895040 | bytes 1384700 | tf_op jit(solution)/shard_map/while/body/eval_jaxpr/jtxy,jky->jtxk/dot_general | solution.py:107
  109.1 1.6 fusion.204
  113.9 1.1 dynamic-slice_bitcast_fusion.6
  115.0 16.0 %fusion.203 = f32[21,8,64,16]{2,3,1,0:T(8,128)S(1)} fusion(f32[8,64,128]{2,1,0:T(8,128)S(1)} %get-tuple-element.566, f32[8,64,128]{2,1,0:T(8,128)S(1)} %get-tuple-element.567, pred[21]{0:T(512)(128)(4,1)S(1)} %get-tuple-element.568, pred[21]{0:T(512)(128)(4,1)S(1)} %get-tuple-element.569, pred[21]{0:T(512)(128)(4,1)S(1)} %get-tuple-element.570, ...), kind=kOutput, calls=%fused_computation.4.clone.1 | convolution fusion | flops 295895040 | bytes 1384700 | tf_op jit(solution)/shard_map/while/body/eval_jaxpr/jtxy,jky->jtxk/dot_general | solution.py:107
  131.0 1.6 fusion.204
  135.8 1.1 dynamic-slice_bitcast_fusion.6
  136.9 16.0 %fusion.203 = f32[21,8,64,16]{2,3,1,0:T(8,128)S(1)} fusion(f32[8,64,128]{2,1,0:T(8,128)S(1)} %get-tuple-element.566, f32[8,64,128]{2,1,0:T(8,128)S(1)} %get-tuple-element.567, pred[21]{0:T(512)(128)(4,1)S(1)} %get-tuple-element.568, pred[21]{0:T(512)(128)(4,1)S(1)} %get-tuple-element.569, pred[21]{0:T(512)(128)(4,1)S(1)} %get-tuple-element.570, ...), kind=kOutput, calls=%fused_computation.4.clone.1 | convolution fusion | flops 295895040 | bytes 1384700 | tf_op jit(solution)/shard_map/while/body/eval_jaxpr/jtxy,jky->jtxk/dot_general | solution.py:107
  152.8 1.6 fusion.204
  157.6 1.1 dynamic-slice_bitcast_fusion.6
  158.7 16.0 %fusion.203 = f32[21,8,64,16]{2,3,1,0:T(8,128)S(1)} fusion(f32[8,64,128]{2,1,0:T(8,128)S(1)} %get-tuple-element.566, f32[8,64,128]{2,1,0:T(8,128)S(1)} %get-tuple-element.567, pred[21]{0:T(512)(128)(4,1)S(1)} %get-tuple-element.568, pred[21]{0:T(512)(128)(4,1)S(1)} %get-tuple-element.569, pred[21]{0:T(512)(128)(4,1)S(1)} %get-tuple-element.570, ...), kind=kOutput, calls=%fused_computation.4.clone.1 | convolution fusion | flops 295895040 | bytes 1384700 | tf_op jit(solution)/shard_map/while/body/eval_jaxpr/jtxy,jky->jtxk/dot_general | solution.py:107
  174.7 1.6 fusion.204
  180.7 7.0 all-to-all-start
  187.6 20.5 %all-to-all-done = f32[16,23,512]{2,1,0:T(8,128)S(1)} async-done(((f32[16,23,512]{2,1,0:T(8,128)}), f32[16,23,512]{2,1,0:T(8,128)S(1)}, u32[]{:S(2)}, u32[]{:S(2)}) %all-to-all-start) | async-done | bytes 753696 | tf_op jit(solution)/shard_map/all_to_all | solution.py:130
  208.4 3.0 all_gather.3
  212.2 2.8 gather_fusion
  216.5 349.0 %pmax.7 = f32[]{:T(128)} all-reduce(f32[]{:T(128)S(6)} %sqrt.28), channel_id=1, replica_groups=mesh['param'=16,'space'=2,'term'=8] {'param','term'}, use_global_device_ids=true, to_apply=%region_5.6 | all-reduce | flops 1 | bytes 8 | tf_op jit(solution)/shard_map/pmax | solution.py:145
  566.5 342.2 %psum.14 = f32[24]{0:T(128)S(1)} all-reduce(f32[24]{0:T(128)S(1)} %convolution_bitcast_fusion.5), channel_id=1, replica_groups=mesh['param'=16,'space'=2,'term'=8] {'param','term'}, use_global_device_ids=true, to_apply=%region_7.8 | all-reduce | flops 24 | bytes 192 | tf_op jit(solution)/shard_map/psum | solution.py:148
  910.7 344.2 %psum.15 = f32[24]{0:T(128)S(1)} all-reduce(f32[24]{0:T(128)S(1)} %convolution_bitcast_fusion.4), channel_id=1, replica_groups=mesh['param'=16,'space'=2,'term'=8] {'param','term'}, use_global_device_ids=true, to_apply=%region_10.11 | all-reduce | flops 24 | bytes 192 | tf_op jit(solution)/shard_map/psum | solution.py:151
  (148 shorter events, 34.9 us)
Async XLA Ops:
  5.7 16.0 %copy-start = (s32[4]{0:T(128)S(1)}, s32[4]{0:T(128)}, u32[]{:S(2)}) copy-start(s32[4]{0:T(128)} %get-tuple-element.619) | copy-start | bytes 52 | tf_op jit(solution)/shard_map/while
  21.7 3.7 copy-start.1
  27.6 16.0 %copy-start = (s32[4]{0:T(128)S(1)}, s32[4]{0:T(128)}, u32[]{:S(2)}) copy-start(s32[4]{0:T(128)} %get-tuple-element.619) | copy-start | bytes 52 | tf_op jit(solution)/shard_map/while
  43.5 3.7 copy-start.1
  49.4 16.0 %copy-start = (s32[4]{0:T(128)S(1)}, s32[4]{0:T(128)}, u32[]{:S(2)}) copy-start(s32[4]{0:T(128)} %get-tuple-element.619) | copy-start | bytes 52 | tf_op jit(solution)/shard_map/while
  65.4 3.7 copy-start.1
  71.3 16.0 %copy-start = (s32[4]{0:T(128)S(1)}, s32[4]{0:T(128)}, u32[]{:S(2)}) copy-start(s32[4]{0:T(128)} %get-tuple-element.619) | copy-start | bytes 52 | tf_op jit(solution)/shard_map/while
  87.2 3.7 copy-start.1
  93.1 16.0 %copy-start = (s32[4]{0:T(128)S(1)}, s32[4]{0:T(128)}, u32[]{:S(2)}) copy-start(s32[4]{0:T(128)} %get-tuple-element.619) | copy-start | bytes 52 | tf_op jit(solution)/shard_map/while
  109.1 3.7 copy-start.1
  115.0 16.0 %copy-start = (s32[4]{0:T(128)S(1)}, s32[4]{0:T(128)}, u32[]{:S(2)}) copy-start(s32[4]{0:T(128)} %get-tuple-element.619) | copy-start | bytes 52 | tf_op jit(solution)/shard_map/while
  131.0 3.7 copy-start.1
  136.8 16.0 %copy-start = (s32[4]{0:T(128)S(1)}, s32[4]{0:T(128)}, u32[]{:S(2)}) copy-start(s32[4]{0:T(128)} %get-tuple-element.619) | copy-start | bytes 52 | tf_op jit(solution)/shard_map/while
  152.8 3.7 copy-start.1
  158.7 16.0 %copy-start = (s32[4]{0:T(128)S(1)}, s32[4]{0:T(128)}, u32[]{:S(2)}) copy-start(s32[4]{0:T(128)} %get-tuple-element.619) | copy-start | bytes 52 | tf_op jit(solution)/shard_map/while
  174.7 3.7 copy-start.1
  180.7 385.7 %copy-start.2 = (s32[168]{0:T(256)S(1)}, s32[168]{0:T(256)}, u32[]{:S(2)}) copy-start(s32[168]{0:T(256)} %param.13) | copy-start | bytes 2020
  180.7 27.5 %all-to-all-start = ((f32[16,23,512]{2,1,0:T(8,128)}), f32[16,23,512]{2,1,0:T(8,128)S(1)}, u32[]{:S(2)}, u32[]{:S(2)}) async-start(f32[16,23,512]{2,1,0:T(8,128)} %bitcast.5), calls=%async_computation | async-start | bytes 1572864 | tf_op jit(solution)/shard_map/all_to_all | solution.py:130
where the time goes:
time: 1260 us
  blocking collectives  1040 us (83%)
  matrix products  157 us (12%)
  local copies, waits for them, and re-layouts  24.8 us (2%)
  waiting for transfers between devices  20.5 us (2%)
    pmax x1, blocking collectives, body(): largest = lax.pmax(jnp.max(frobenius), ('param', 'term'))  349 us
    psum x1, blocking collectives, body(): second_sq = lax.psum(group_squares(second_guess, onehot), ('param', 'term'))  344 us
    psum x1, blocking collectives, body(): first_sq = lax.psum(group_squares(first_guess, onehot), ('param', 'term'))  342 us
    dot_general x8, matrix products, tile_integrals(): across_y = jnp.einsum('jtxy,jky->jtxk', monomial, y_pick, precision=highest)  128 us
  transfers between devices with their start and end apart: 1, of which 1 were waited for; matrix products, arithmetic and copies ran while one was open for 0% of the time, Pallas kernels for 0%

commit v1 on v0

--- a/solution.py
+++ b/solution.py
@@ -145,7 +145,9 @@
     largest = lax.pmax(jnp.max(frobenius), ("param", "term"))
     step_size = 1.0 / largest
     first_guess = step_size * right_side
-    first_sq = lax.psum(group_squares(first_guess, onehot), ("param", "term"))
+    first_sq = jnp.sum(
+        lax.all_gather(group_squares(first_guess, onehot), ("param", "term")), axis=0
+    )
     first = shrink(first_guess, first_sq, onehot)
     second_guess = first - step_size * (correlate(correlation, first) - right_side)
     second_sq = lax.psum(group_squares(second_guess, onehot), ("param", "term"))

time: 1260 us -> 1600 us (1.27)
  blocking collectives: 1040 us -> 1380 us
    unnamed x0 -> x1, blocking collectives: none -> 682 us
    psum x1 -> x0, blocking collectives: 342 us -> none  [body(): first_sq = lax.psum(group_squares(first_guess, onehot), ('param', 'term'))]
where the time goes in v1:
time: 1600 us
  blocking collectives  1380 us (86%)
  matrix products  157 us (10%)
  local copies, waits for them, and re-layouts  25.7 us (2%)
  waiting for transfers between devices  19.3 us (1%)
    unnamed x1, blocking collectives  682 us
    pmax x1, blocking collectives, body(): largest = lax.pmax(jnp.max(frobenius), ('param', 'term'))  349 us
    psum x1, blocking collectives, body(): second_sq = lax.psum(group_squares(second_guess, onehot), ('param', 'term'))  342 us
    dot_general x8, matrix products, tile_integrals(): across_y = jnp.einsum('jtxy,jky->jtxk', monomial, y_pick, precision=highest)  128 us
  transfers between devices with their start and end apart: 1, of which 1 were waited for; matrix products, arithmetic and copies ran while one was open for 0% of the time, Pallas kernels for 0%

profile of v1, /device:TPU:0, one launch (start us, length us, event | category | flops | bytes accessed | tf_op | source)
XLA Modules:
  0.0 1595.7 jit_solution(12817031866487683375)
XLA Ops:
  4.6 175.0 %while.18 = (s32[]{:T(128)}, f32[2,8,23,512]{3,0,2,1:T(2,128)S(1)}, s32[21,1]{0,1:T(1,128)S(1)}, f32[8,2,8,64,128]{4,3,2,1,0:T(8,128)}, s32[21,1]{0,1:T(1,128)S(...) while((s32[]{:T(128)}, f32[2,8,23,512]{3,0,2,1:T(2,128)S(1)}, ...), condition=%wide.region_1.2_spmd.clone.clone, body=%wide.region_0.1_spmd.clone.clone.sunk | while | flops 324181856 | bytes 4605749 | solution.py:129
  4.6 1.1 dynamic-slice_bitcast_fusion.6
  5.7 16.0 fusion.203
  21.7 1.6 fusion.204
  26.5 1.1 dynamic-slice_bitcast_fusion.6
  27.6 16.0 fusion.203
  43.6 1.6 fusion.204
  48.4 1.1 dynamic-slice_bitcast_fusion.6
  49.4 16.0 fusion.203
  65.4 1.6 fusion.204
  70.2 1.1 dynamic-slice_bitcast_fusion.6
  71.3 16.0 fusion.203
  87.3 1.6 fusion.204
  92.1 1.1 dynamic-slice_bitcast_fusion.6
  93.2 16.0 fusion.203
  109.1 1.6 fusion.204
  113.9 1.1 dynamic-slice_bitcast_fusion.6
  115.0 16.0 fusion.203
  131.0 1.6 fusion.204
  135.8 1.1 dynamic-slice_bitcast_fusion.6
  136.9 16.0 fusion.203
  152.8 1.6 fusion.204
  157.6 1.1 dynamic-slice_bitcast_fusion.6
  158.7 16.0 fusion.203
  174.7 1.6 fusion.204
  180.7 7.0 all-to-all-start
  188.9 19.3 %all-to-all-done = f32[16,23,512]{2,1,0:T(8,128)S(1)} async-done(((f32[16,23,512]{2,1,0:T(8,128)}), f32[16,23,512]{2,1,0:T(8,128)S(1)}, u32[]{:S(2)}, u32[]{:S(2)}) %all-to-all-start) | async-done | bytes 753696 | tf_op jit(solution)/shard_map/all_to_all | solution.py:130
  208.4 3.0 all_gather.9
  212.2 2.8 gather_fusion
  216.5 349.0 %pmax.7 = f32[]{:T(128)} all-reduce(f32[]{:T(128)S(6)} %sqrt.28), channel_id=1, replica_groups=mesh['param'=16,'space'=2,'term'=8] {'param','term'}, use_global_device_ids=true, to_apply=%region_5.6 | all-reduce | flops 1 | bytes 8 | tf_op jit(solution)/shard_map/pmax | solution.py:145
  566.8 681.6 %all-reduce = f32[3072]{0:T(1024)S(1)} all-reduce(f32[3072]{0:T(1024)S(1)} %dynamic-update-slice), channel_id=2, replica_groups=mesh['param'=16,'space'=2,'term'=8] {'param','term'}, use_global_device_ids=true, to_apply=%add | all-reduce | flops 3072 | bytes 24576
  1250.5 342.2 %psum.7 = f32[24]{0:T(128)S(1)} all-reduce(f32[24]{0:T(128)S(1)} %convolution_bitcast_fusion.4), channel_id=1, replica_groups=mesh['param'=16,'space'=2,'term'=8] {'param','term'}, use_global_device_ids=true, to_apply=%region_10.11 | all-reduce | flops 24 | bytes 192 | tf_op jit(solution)/shard_map/psum | solution.py:153
  (155 shorter events, 35.9 us)
Async XLA Ops:
  4.6 183.1 %copy-start.3 = (u32[256]{0:T(256)S(1)}, u32[256]{0:T(256)}, u32[]{:S(2)}) copy-start(u32[256]{0:T(256)} %constant.300) | copy-start | bytes 3076
  5.7 16.0 %copy-start = (s32[4]{0:T(128)S(1)}, s32[4]{0:T(128)}, u32[]{:S(2)}) copy-start(s32[4]{0:T(128)} %get-tuple-element.619) | copy-start | bytes 52 | tf_op jit(solution)/shard_map/while
  21.7 3.7 copy-start.1
  27.6 16.0 %copy-start = (s32[4]{0:T(128)S(1)}, s32[4]{0:T(128)}, u32[]{:S(2)}) copy-start(s32[4]{0:T(128)} %get-tuple-element.619) | copy-start | bytes 52 | tf_op jit(solution)/shard_map/while
  43.5 3.7 copy-start.1
  49.4 16.0 %copy-start = (s32[4]{0:T(128)S(1)}, s32[4]{0:T(128)}, u32[]{:S(2)}) copy-start(s32[4]{0:T(128)} %get-tuple-element.619) | copy-start | bytes 52 | tf_op jit(solution)/shard_map/while
  65.4 3.7 copy-start.1
  71.3 16.0 %copy-start = (s32[4]{0:T(128)S(1)}, s32[4]{0:T(128)}, u32[]{:S(2)}) copy-start(s32[4]{0:T(128)} %get-tuple-element.619) | copy-start | bytes 52 | tf_op jit(solution)/shard_map/while
  87.3 3.7 copy-start.1
  93.1 16.0 %copy-start = (s32[4]{0:T(128)S(1)}, s32[4]{0:T(128)}, u32[]{:S(2)}) copy-start(s32[4]{0:T(128)} %get-tuple-element.619) | copy-start | bytes 52 | tf_op jit(solution)/shard_map/while
  109.1 3.7 copy-start.1
  115.0 16.0 %copy-start = (s32[4]{0:T(128)S(1)}, s32[4]{0:T(128)}, u32[]{:S(2)}) copy-start(s32[4]{0:T(128)} %get-tuple-element.619) | copy-start | bytes 52 | tf_op jit(solution)/shard_map/while
  131.0 3.7 copy-start.1
  136.9 16.0 %copy-start = (s32[4]{0:T(128)S(1)}, s32[4]{0:T(128)}, u32[]{:S(2)}) copy-start(s32[4]{0:T(128)} %get-tuple-element.619) | copy-start | bytes 52 | tf_op jit(solution)/shard_map/while
  152.8 3.7 copy-start.1
  158.7 16.0 %copy-start = (s32[4]{0:T(128)S(1)}, s32[4]{0:T(128)}, u32[]{:S(2)}) copy-start(s32[4]{0:T(128)} %get-tuple-element.619) | copy-start | bytes 52 | tf_op jit(solution)/shard_map/while
  174.7 3.7 copy-start.1
  180.7 385.7 %copy-start.2 = (s32[168]{0:T(256)S(1)}, s32[168]{0:T(256)}, u32[]{:S(2)}) copy-start(s32[168]{0:T(256)} %param.13) | copy-start | bytes 2020
  180.7 27.5 %all-to-all-start = ((f32[16,23,512]{2,1,0:T(8,128)}), f32[16,23,512]{2,1,0:T(8,128)S(1)}, u32[]{:S(2)}, u32[]{:S(2)}) async-start(f32[16,23,512]{2,1,0:T(8,128)} %bitcast.5), calls=%async_computation | async-start | bytes 1572864 | tf_op jit(solution)/shard_map/all_to_all | solution.py:130
